TPU v7x, 256 devices: a whole 4x4x8 slice. The times are simulated.
256 devices in a mesh: dp: 4 (over z_hi, core), ctx: 16 (over z_lo, y), tp: 4 (over x).
Axes of the slice: x: 4, y: 4, z: 8 (z_hi: 2, z_lo: 4; z = z_hi * 4 + z_lo), core: 2. Of those that a mesh axis runs over, the one named last changes fastest.
Arguments:
- teacher_part: bfloat16 [4, 4, 4096, 8192], P('dp', 'tp', 'ctx'), may hold values from -8 to 8
- student_in: bfloat16 [4, 4096, 4096], P('dp', 'ctx'), may hold values from -24 to 24
- out_proj: bfloat16 [4096, 4096], P('ctx', 'tp'), may hold values from -0.09375 to 0.09375
- segment_ids: int32 [4, 4096], P('dp'), may hold values from 0 to 7, never falling along the last dimension, each value on 1 to 1024 neighbouring positions
- valid_count: int32 [4], P('dp'), may hold values from 256 to 4096, as said below
Outputs:
- doc_loss: float32 [4], P('dp')
- wo_grad: float32 [4096, 4096], P('ctx', 'tp')
- state_grad: float32 [4, 4096, 4096], P('dp', 'ctx', 'tp')
Inputs may be any that keep to these rules, and one draw needn't show every extreme that they name: `valid_count`: one document in every draw is valid at all 4096 positions. `segment_ids`: segment numbers never fall along a document.
All inputs are finite; a program needn't handle non-finite values.
Results may differ from a plain program's by a relative error of at most 0.019.
The roundings to bfloat16 on the way count: a program that leaves them out, or rounds other values in their place, can miss the bound.
Values may be sent and summed in bfloat16 or wider, within the bound.
A program may use at most 64 MiB of HBM per device.

v0:
```python
import math
import jax
import jax.numpy as jnp
from jax import lax
from jax.sharding import PartitionSpec as P

DS = 4096
HEADS = 32
masked_score = -1e30


def shifted_2(value, axis, steps):
    count = lax.axis_size(axis)
    leading, last = (max(0, -steps), min(count, count - steps))
    return lax.ppermute(value, axis, [(source, source + steps) for source in range(leading, last)])


def log_probs(scores, allowed):
    scores = jnp.where(allowed[None, :, :], scores, masked_score)
    top = jnp.max(scores, axis=-1, keepdims=True)
    shifted = scores - top
    return shifted - jnp.log(jnp.sum(jnp.exp(shifted), axis=-1, keepdims=True))


def window_terms(
    teacher_query, teacher_keys, student_query, student_keys, allowed, live, head_count
):
    length = teacher_query.shape[0]
    teacher_qh = teacher_query.reshape(length, head_count, -1)
    teacher_kh = teacher_keys.reshape(2 * length, head_count, -1)
    student_qh = student_query.reshape(length, head_count, -1)
    student_kh = student_keys.reshape(2 * length, head_count, -1)
    teacher_scale = 1.0 / math.sqrt(teacher_qh.shape[-1])
    student_scale = 1.0 / math.sqrt(student_qh.shape[-1])
    teacher_scores = (
        jnp.einsum("qhd,khd->hqk", teacher_qh, teacher_kh, preferred_element_type=jnp.float32)
        * teacher_scale
    )
    student_scores = (
        jnp.einsum("qhd,khd->hqk", student_qh, student_kh, preferred_element_type=jnp.float32)
        * student_scale
    )
    teacher_logp = log_probs(teacher_scores, allowed)
    student_logp = log_probs(student_scores, allowed)
    teacher_prob = jnp.exp(teacher_logp)
    student_prob = jnp.exp(student_logp)
    divergence = jnp.sum(teacher_prob * (teacher_logp - student_logp), axis=-1)
    loss_part = jnp.sum(divergence * live[None, :]) / HEADS
    grad_scale = live[None, :, None] * (student_scale / HEADS)
    score_grad = ((student_prob - teacher_prob) * grad_scale).astype(jnp.bfloat16)
    query_grad = jnp.einsum(
        "hqk,khd->qhd", score_grad, student_kh, preferred_element_type=jnp.float32
    ).reshape(length, -1)
    key_grad = jnp.einsum(
        "hqk,qhd->khd", score_grad, student_qh, preferred_element_type=jnp.float32
    ).reshape(2 * length, -1)
    return (loss_part, query_grad, key_grad)


def per_device(teacher_part, student_in, out_proj, segment_ids, valid_count):
    window_len = student_in.shape[1]
    head_count = HEADS // lax.axis_size("tp")
    unscale = HEADS * math.sqrt(DS // HEADS)
    partial_sum = teacher_part[0, 0].astype(jnp.float32)
    teacher_own = lax.psum_scatter(
        partial_sum.astype(jnp.bfloat16), "tp", scatter_dimension=1, tiled=True
    )
    tokens = student_in[0]
    columns = tokens
    student_own = jnp.dot(
        columns,
        lax.all_gather(out_proj, "ctx", axis=0, tiled=True),
        preferred_element_type=jnp.float32,
    ).astype(jnp.bfloat16)
    teacher_prev, student_prev = shifted_2((teacher_own, student_own), "ctx", 1)
    teacher_keys = jnp.concatenate([teacher_prev, teacher_own], 0)
    student_keys = jnp.concatenate([student_prev, student_own], 0)
    window = lax.axis_index("ctx")
    start = window * window_len
    segments = segment_ids[0]
    segment_padded = jnp.concatenate([jnp.full((window_len,), -1, jnp.int32), segments], 0)
    query_segment = lax.dynamic_slice_in_dim(segments, start, window_len, 0)
    key_segment = lax.dynamic_slice_in_dim(segment_padded, start, 2 * window_len, 0)
    valid_limit = valid_count[0]
    query_position = start + jnp.arange(window_len, dtype=jnp.int32)
    key_position = start - window_len + jnp.arange(2 * window_len, dtype=jnp.int32)
    allowed = (key_segment[None, :] == query_segment[:, None]) & (
        key_position[None, :] < valid_limit
    )
    live = jnp.where(query_position < valid_limit, 1.0, 0.0).astype(jnp.float32)
    loss_part, query_grad, key_grad = window_terms(
        teacher_own, teacher_keys, student_own, student_keys, allowed, live, head_count
    )
    from_next = shifted_2(key_grad[:window_len].astype(jnp.bfloat16), "ctx", -1).astype(jnp.float32)
    hidden_grad = (query_grad + key_grad[window_len:] + from_next).astype(jnp.bfloat16)
    state_grad = (hidden_grad.astype(jnp.float32) * unscale)[None]
    columns = tokens
    grad_piece = lax.psum_scatter(
        jnp.einsum("tr,tc->rc", columns, hidden_grad, preferred_element_type=jnp.float32).astype(
            jnp.bfloat16
        ),
        "ctx",
        scatter_dimension=0,
        tiled=True,
    )
    wo_grad = lax.psum(grad_piece, "dp").astype(jnp.float32)
    doc_loss = lax.psum(loss_part, ("ctx", "tp"))
    return (doc_loss.reshape(1), wo_grad, state_grad)


def solution(mesh):
    return jax.shard_map(
        per_device,
        mesh=mesh,
        in_specs=(
            P("dp", "tp", "ctx", None),
            P("dp", "ctx", None),
            P("ctx", "tp"),
            P("dp", None),
            P("dp"),
        ),
        out_specs=(P("dp"), P("ctx", "tp"), P("dp", "ctx", "tp")),
        check_vma=False,
    )
```

profile of v0, /device:TPU:0, one launch (start us, length us, event | category | flops | bytes accessed | tf_op | source)
XLA Modules:
  0.0 515.2 jit_solution(8294521861776870635)
XLA Ops:
  8.0 0.0 copy-start
  8.0 0.0 reduce-scatter.3.cloned.1.call-start
  8.1 6.5 %copy.32 = bf16[1,1,256,8192]{2,3,1,0:T(8,128)(2,1)} copy(bf16[1,1,256,8192]{3,2,1,0:T(8,128)(2,1)} %param.5) | data formatting | bytes 8388608 | tf_op args[0]
  14.6 0.0 copy-start.4
  14.6 0.0 reduce-scatter.3.cloned.1.call-update
  14.6 0.0 all-gather.2.cloned.1.call-start
  14.6 0.5 all-gather.2.cloned.1.call-update
  15.2 0.0 reduce-scatter.5.cloned.1.call-start
  15.2 50.1 %reduce-scatter.3.cloned.1.call-done = bf16[256,2048]{0,1:T(8,128)(2,1)} async-done(((bf16[256,8192]{0,1:T(8,128)(2,1)}), bf16[256,2048]{0,1:T(8,128)(2,1)}) %reduce-scatter.3.cloned.1.call-update) | async-done | bytes 1048592 | tf_op jit(solution)/shard_map/reduce_scatter | solution.py:65
  65.4 3.5 collective-permute-start
  69.5 0.0 copy-done.4
  69.5 0.1 pad_dynamic-slice_fusion
  69.6 0.2 compare_and_fusion
  69.8 44.8 %collective-permute-done = bf16[256,2048]{0,1:T(8,128)(2,1)S(1)} collective-permute-done((bf16[256,2048]{0,1:T(8,128)(2,1)}, bf16[256,2048]{0,1:T(8,128)(2,1)S(1)}, u32[]{:S(2)}, u32[]{:S(2)}) %collective-permute-start) | collective-permute-done | bytes 1048608 | tf_op jit(solution)/shard_map/ppermute | solution.py:15
  114.6 2.8 pad_maximum_fusion
  117.4 23.7 %all-gather.2.cloned.1.call-done = bf16[4096,1024]{1,0:T(8,128)(2,1)} async-done(((bf16[256,1024]{1,0:T(8,128)(2,1)}), bf16[4096,1024]{1,0:T(8,128)(2,1)}) %all-gather.2.cloned.1.call-update) | async-done | bytes 8388624 | tf_op jit(solution)/shard_map/all_gather | solution.py:72
  141.2 0.0 copy-done
  141.2 5.7 %fusion.24 = bf16[256,1024]{1,0:T(8,128)(2,1)S(1)} fusion(bf16[4096,1024]{1,0:T(8,128)(2,1)} %all-gather.2.cloned.1.call-done, bf16[1,256,4096]{2,1,0:T(8,128)(2,1)S(1)} %copy-done), kind=kOutput, calls=%fused_computation.32 | convolution fusion | flops 2147745792 | bytes 11010048 | tf_op jit(solution)/shard_map/dot_general | solution.py:70
  146.9 3.1 collective-permute-start.1
  150.0 5.2 %fusion.8 = f32[8,256,512]{1,2,0:T(8,128)} fusion(pred[256,512]{0,1:T(8,128)(4,1)S(1)} %compare_and_fusion, bf16[512,8,256]{0,2,1:T(8,128)(2,1)} %bitcast.58, bf16[256,8,256]{0,2,1:T(8,128)(2,1)} %bitcast.60), kind=kOutput, calls=%fused_computation.17 | convolution fusion | flops 540019200 | bytes 7471104 | tf_op jit(solution)/shard_map/sub | solution.py:21
  155.2 6.2 %log_subtract_fusion.1 = f32[8,256,512]{1,2,0:T(8,128)} fusion(f32[8,256,512]{1,2,0:T(8,128)} %fusion.8), kind=kOutput, calls=%fused_computation.6 | output fusion | flops 1051135 | bytes 8388608 | tf_op jit(solution)/shard_map/reduce_sum | solution.py:22
  161.4 1.0 copy.50
  162.4 0.0 collective-permute-done.1
  162.4 1.0 pad_maximum_fusion.1
  163.4 1.5 copy.51
  164.9 4.3 fusion.6
  169.2 7.2 %multiply_convert_fusion = (bf16[8,256,512]{1,2,0:T(8,128)(2,1)S(1)}, f32[8,256]{1,0:T(8,128)S(1)}) fusion(f32[8,256,512]{1,2,0:T(8,128)} %log_subtract_fusion.1, f32[256]{0:T(256)S(1)} %get-tuple-element.15, f32[8,256,512]{1,2,0:T(8,128)} %fusion.6), kind=kOutput, calls=%fused_computation.8 | output fusion | flops 7340543 | bytes 10494976 | tf_op jit(solution)/shard_map/reduce_sum | solution.py:22
  176.4 0.0 copy-start.1
  176.4 1.3 copy-done.1
  177.8 0.0 copy-done.3
  177.8 0.8 convolution_bitcast_fusion
  178.6 0.0 copy-start.2
  178.6 1.3 copy-done.2
  179.9 0.9 slice.15
  180.7 2.0 copy.42
  182.8 1.5 collective-permute-start.2
  184.2 3.3 fusion.23
  187.5 1.6 copy.43
  189.1 8.7 %collective-permute-done.2 = bf16[256,1024]{1,0:T(8,128)(2,1)} collective-permute-done((bf16[256,1024]{1,0:T(8,128)(2,1)}, bf16[256,1024]{1,0:T(8,128)(2,1)}, u32[]{:S(2)}, u32[]{:S(2)}) %collective-permute-start.2) | collective-permute-done | bytes 524320 | tf_op jit(solution)/shard_map/ppermute | solution.py:15
  197.8 6.7 %convert_bitcast_fusion = bf16[4096,1024]{0,1:T(8,128)(2,1)} fusion(bf16[1,256,4096]{2,1,0:T(8,128)(2,1)S(1)} %copy-done, f32[256,1024]{1,0:T(8,128)S(1)} %copy.43, bf16[256,1024]{1,0:T(8,128)(2,1)} %collective-permute-done.2), kind=kOutput, calls=%fused_computation.4 | convolution fusion | flops 2152464384 | bytes 12058624 | tf_op jit(solution)/shard_map/tr,tc->rc/dot_general | solution.py:99
  204.5 0.0 reduce-scatter.5.cloned.1.call-update
  204.5 0.0 all-reduce.3.cloned.1.call-start
  204.6 110.2 %reduce-scatter.5.cloned.1.call-done = bf16[256,1024]{0,1:T(8,128)(2,1)} async-done(((bf16[4096,1024]{0,1:T(8,128)(2,1)}), bf16[256,1024]{0,1:T(8,128)(2,1)}) %reduce-scatter.5.cloned.1.call-update) | async-done | bytes 524304 | tf_op jit(solution)/shard_map/reduce_scatter | solution.py:98
  314.8 0.0 all-reduce.3.cloned.1.call-update
  314.8 0.6 multiply_reduce_fusion.1
  316.1 187.3 %psum.14 = f32[1]{0:T(128)} all-reduce(f32[1]{0:T(128)} %bitcast.8), channel_id=1, replica_groups=mesh['dp'=4,'ctx'=16,'tp'=4] {'ctx','tp'}, use_global_device_ids=true, to_apply=%region_7.8 | all-reduce | flops 1 | bytes 8 | tf_op jit(solution)/shard_map/psum | solution.py:107
  503.4 2.2 multiply_bitcast_fusion
  505.5 2.2 copy.44
  (5 shorter events, 0.0 us)
Async XLA Ops:
  8.0 133.2 %copy-start = (bf16[1,256,4096]{2,1,0:T(8,128)(2,1)S(1)}, bf16[1,256,4096]{2,1,0:T(8,128)(2,1)}, u32[]{:S(2)}) copy-start(bf16[1,256,4096]{2,1,0:T(8,128)(2,1)} %param.6) | copy-start | bytes 6291460
  8.0 57.3 %reduce-scatter.3.cloned.1.call-start = ((), (), s32[]{:S(2)}) async-start(), calls=%async_computation.2 | async-start | bytes 5242880 | tf_op jit(solution)/shard_map/reduce_scatter | solution.py:65
  14.6 54.9 %copy-start.4 = (s32[1,4096]{1,0:T(1,128)S(1)}, s32[1,4096]{1,0:T(1,128)}, u32[]{:S(2)}) copy-start(s32[1,4096]{1,0:T(1,128)} %param.8) | copy-start | bytes 49156
  14.6 126.6 %all-gather.2.cloned.1.call-start = ((), (), s32[]{:S(2)}) async-start(), calls=%async_computation.3 | async-start | bytes 8912896 | tf_op jit(solution)/shard_map/all_gather | solution.py:72
  15.2 299.6 %reduce-scatter.5.cloned.1.call-start = ((), (), s32[]{:S(2)}) async-start(), calls=%async_computation.4 | async-start | bytes 8912896 | tf_op jit(solution)/shard_map/reduce_scatter | solution.py:98
  65.4 49.3 %collective-permute-start = (bf16[256,2048]{0,1:T(8,128)(2,1)}, bf16[256,2048]{0,1:T(8,128)(2,1)S(1)}, u32[]{:S(2)}, u32[]{:S(2)}) collective-permute-start(bf16[256,2048]{0,1:T(8,128)(2,1)} %reduce-scatter.3.cloned.1.call-done), channel_id=1, source_target_pairs={{0,4},{4,8},{8,12},{12,16},{16,20},{20,24},{24,28},{28,32},{32,36}... | collective-permute-start | bytes 3145736 | tf_op jit(solution)/shard_map/ppermute | solution.py:15
  146.9 15.5 %collective-permute-start.1 = (bf16[256,1024]{1,0:T(8,128)(2,1)S(1)}, bf16[256,1024]{1,0:T(8,128)(2,1)S(1)}, u32[]{:S(2)}, u32[]{:S(2)}) collective-permute-start(bf16[256,1024]{1,0:T(8,128)(2,1)S(1)} %fusion.24), channel_id=1, source_target_pairs={{0,4},{4,8},{8,12},{12,16},{16,20},{20,24},{24,28},{28,32},{32,36}... | collective-permute-start | bytes 1572872 | tf_op jit(solution)/shard_map/ppermute | solution.py:15
  169.2 8.6 %copy-start.3 = (bf16[256,1024]{0,1:T(8,128)(2,1)S(1)}, bf16[256,1024]{0,1:T(8,128)(2,1)}, u32[]{:S(2)}) copy-start(bf16[256,1024]{0,1:T(8,128)(2,1)} %copy.50) | copy-start | bytes 1572868
  176.4 1.4 copy-start.1
  178.6 1.3 copy-start.2
  182.8 15.1 %collective-permute-start.2 = (bf16[256,1024]{1,0:T(8,128)(2,1)}, bf16[256,1024]{1,0:T(8,128)(2,1)}, u32[]{:S(2)}, u32[]{:S(2)}) collective-permute-start(bf16[256,1024]{1,0:T(8,128)(2,1)} %copy.42), channel_id=1, source_target_pairs={{4,0},{8,4},{12,8},{16,12},{20,16},{24,20},{28,24},{32,28},{36,32}... | collective-permute-start | bytes 1572872 | tf_op jit(solution)/shard_map/ppermute | solution.py:15
  204.5 301.0 %all-reduce.3.cloned.1.call-start = ((), (), s32[]{:S(2)}) async-start(), calls=%async_computation.5 | async-start | bytes 1048576 | tf_op jit(solution)/shard_map/psum | solution.py:106
Sparse Core Ops, SparseCore 0:
  14.7 50.6 reduce-scatter.2
  314.9 54.1 all-reduce.2
Sparse Core Ops, SparseCore 1:
  16.9 124.3 all-gather.1
  204.6 110.1 reduce-scatter.4
where the time goes:
time: 516 us; the launch traced here: 515 us
  waiting for transfers between devices  238 us (46%)
  blocking collectives  187 us (36%)
  matrix products  25.9 us (5%)
  other arithmetic  20.2 us (4%)
  local copies, waits for them, and re-layouts  18.4 us (4%)
  between operations  16.9 us (3%)
  starting transfers between devices  8.2 us (2%)
    psum x1, blocking collectives, per_device(): doc_loss = lax.psum(loss_part, ('ctx', 'tp'))  187 us
    reduce_scatter x1, waiting for transfers between devices, per_device(): lax.psum_scatter(jnp.einsum('tr,tc->rc', columns, hidden_grad, preferred_...  110 us
    ppermute x3, waiting for transfers between devices, shifted_2(): lax.ppermute(value, axis, [(source, source + steps) for source in range(l...  53.5 us
    reduce_scatter x1, waiting for transfers between devices, per_device(): lax.psum_scatter(partial_sum.astype(jnp.bfloat16), 'tp', scatter_dimensio...  50.1 us
    all_gather x1, waiting for transfers between devices, per_device(): lax.all_gather(out_proj, 'ctx', axis=0, tiled=True)  23.7 us
    reduce_sum x2, other arithmetic, log_probs(): return shifted - jnp.log(jnp.sum(jnp.exp(shifted), axis=-1, keepdims=True))  13.4 us
    unnamed x12, local copies, waits for them, and re-layouts  11.4 us
  transfers between devices with their start and end apart: 7, of which 5 were waited for; matrix products, arithmetic and copies ran while one was open for 4% of the time, Pallas kernels for 0%

commit v1 on v0

--- a/solution.py
+++ b/solution.py
@@ -69,7 +69,9 @@
     columns = tokens
     student_own = jnp.dot(
         columns,
-        lax.all_gather(out_proj, "ctx", axis=0, tiled=True),
+        jnp.concatenate(
+            lax.all_to_all(jnp.stack([out_proj] * lax.axis_size("ctx")), "ctx", 0, 0), axis=0
+        ),
         preferred_element_type=jnp.float32,
     ).astype(jnp.bfloat16)
     teacher_prev, student_prev = shifted_2((teacher_own, student_own), "ctx", 1)

time: 516 us -> 603 us (1.17)
  waiting for transfers between devices: 238 us -> 314 us
  starting transfers between devices: 8.2 us -> 14.5 us
    reduce_scatter x1, waiting for transfers between devices: 110 us -> 157 us  [per_device(): lax.psum_scatter(jnp.einsum('tr,tc->rc', columns, hidden_grad, preferred_...]
    all_to_all x0 -> x1, waiting for transfers between devices: none -> 36.5 us  [per_device(): lax.all_to_all(jnp.stack([out_proj] * lax.axis_size('ctx')), 'ctx', 0, 0)]
    all_gather x1 -> x0, waiting for transfers between devices: 23.7 us -> none  [per_device(): lax.all_gather(out_proj, 'ctx', axis=0, tiled=True)]
    ppermute x3, waiting for transfers between devices: 53.5 us -> 70.6 us  [shifted_2(): lax.ppermute(value, axis, [(source, source + steps) for source in range(l...]
    all_to_all x0 -> x1, starting transfers between devices: none -> 6.98 us  [per_device(): lax.all_to_all(jnp.stack([out_proj] * lax.axis_size('ctx')), 'ctx', 0, 0)]
  transfers between devices with their start and end apart: 7 -> 7, of which waited for: 5 -> 5; matrix products, arithmetic and copies ran while one was open for 4% -> 5% of each run, Pallas kernels for 0% -> 0%
where the time goes in v1:
time: 603 us; the launch traced here: 602 us
  waiting for transfers between devices  314 us (52%)
  blocking collectives  189 us (31%)
  matrix products  25.9 us (4%)
  local copies, waits for them, and re-layouts  23.8 us (4%)
  other arithmetic  20.1 us (3%)
  between operations  15.2 us (3%)
  starting transfers between devices  14.5 us (2%)
    psum x1, blocking collectives, per_device(): doc_loss = lax.psum(loss_part, ('ctx', 'tp'))  189 us
    reduce_scatter x1, waiting for transfers between devices, per_device(): lax.psum_scatter(jnp.einsum('tr,tc->rc', columns, hidden_grad, preferred_...  157 us
    ppermute x3, waiting for transfers between devices, shifted_2(): lax.ppermute(value, axis, [(source, source + steps) for source in range(l...  70.6 us
    reduce_scatter x1, waiting for transfers between devices, per_device(): lax.psum_scatter(partial_sum.astype(jnp.bfloat16), 'tp', scatter_dimensio...  49.9 us
    all_to_all x1, waiting for transfers between devices, per_device(): lax.all_to_all(jnp.stack([out_proj] * lax.axis_size('ctx')), 'ctx', 0, 0)  36.5 us
    reduce_sum x2, other arithmetic, log_probs(): return shifted - jnp.log(jnp.sum(jnp.exp(shifted), axis=-1, keepdims=True))  13.4 us
  transfers between devices with their start and end apart: 7, of which 5 were waited for; matrix products, arithmetic and copies ran while one was open for 5% of the time, Pallas kernels for 0%

profile of v1, /device:TPU:0, one launch (start us, length us, event | category | flops | bytes accessed | tf_op | source)
XLA Modules:
  0.0 602.0 jit_solution(9601057607871902753)
XLA Ops:
  7.2 0.0 copy-start
  7.2 5.5 stack.2
  12.7 7.0 %all-to-all-start = ((bf16[16,256,1024]{2,1,0:T(8,128)(2,1)}), bf16[16,256,1024]{2,1,0:T(8,128)(2,1)}, u32[]{:S(2)}, u32[]{:S(2)}) async-start(bf16[16,256,1024]{2,1,0:T(8,128)(2,1)} %stack.2), calls=%async_computation.1 | async-start | bytes 16777216 | tf_op jit(solution)/shard_map/all_to_all | solution.py:73
  19.6 0.0 reduce-scatter.3.cloned.1.call-start
  19.7 6.4 %copy.32 = bf16[1,1,256,8192]{2,3,1,0:T(8,128)(2,1)} copy(bf16[1,1,256,8192]{3,2,1,0:T(8,128)(2,1)} %param.5) | data formatting | bytes 8388608 | tf_op args[0]
  26.1 0.0 copy-start.4
  26.1 0.0 reduce-scatter.3.cloned.1.call-update
  26.1 0.0 reduce-scatter.5.cloned.1.call-start
  26.2 49.9 %reduce-scatter.3.cloned.1.call-done = bf16[256,2048]{0,1:T(8,128)(2,1)} async-done(((bf16[256,8192]{0,1:T(8,128)(2,1)}), bf16[256,2048]{0,1:T(8,128)(2,1)}) %reduce-scatter.3.cloned.1.call-update) | async-done | bytes 1048592 | tf_op jit(solution)/shard_map/reduce_scatter | solution.py:65
  76.1 3.4 collective-permute-start
  80.2 0.0 copy-done.4
  80.3 0.1 pad_dynamic-slice_fusion
  80.4 0.2 compare_and_fusion
  80.6 52.7 %collective-permute-done = bf16[256,2048]{0,1:T(8,128)(2,1)S(1)} collective-permute-done((bf16[256,2048]{0,1:T(8,128)(2,1)}, bf16[256,2048]{0,1:T(8,128)(2,1)S(1)}, u32[]{:S(2)}, u32[]{:S(2)}) %collective-permute-start) | collective-permute-done | bytes 1048608 | tf_op jit(solution)/shard_map/ppermute | solution.py:15
  133.3 2.7 pad_maximum_fusion
  136.0 36.5 %all-to-all-done = bf16[16,256,1024]{2,1,0:T(8,128)(2,1)} async-done(((bf16[16,256,1024]{2,1,0:T(8,128)(2,1)}), bf16[16,256,1024]{2,1,0:T(8,128)(2,1)}, u32[]{:S(2)}, u32[]{:S(2)}) %all-to-all-start) | async-done | bytes 8388640 | tf_op jit(solution)/shard_map/all_to_all | solution.py:73
  172.5 0.0 copy-done
  172.5 5.7 fusion.24
  178.2 2.5 collective-permute-start.1
  180.7 5.2 fusion.8
  185.8 6.2 %log_subtract_fusion.1 = f32[8,256,512]{1,2,0:T(8,128)} fusion(f32[8,256,512]{1,2,0:T(8,128)} %fusion.8), kind=kOutput, calls=%fused_computation.6 | output fusion | flops 1051135 | bytes 8388608 | tf_op jit(solution)/shard_map/reduce_sum | solution.py:22
  192.1 1.0 copy.50
  193.1 0.0 collective-permute-done.1
  193.1 1.0 pad_maximum_fusion.1
  194.1 1.5 copy.51
  195.6 4.3 fusion.6
  199.9 7.2 %multiply_convert_fusion = (bf16[8,256,512]{1,2,0:T(8,128)(2,1)S(1)}, f32[8,256]{1,0:T(8,128)S(1)}) fusion(f32[8,256,512]{1,2,0:T(8,128)} %log_subtract_fusion.1, f32[256]{0:T(256)S(1)} %get-tuple-element.15, f32[8,256,512]{1,2,0:T(8,128)} %fusion.6), kind=kOutput, calls=%fused_computation.8 | output fusion | flops 7340543 | bytes 10494976 | tf_op jit(solution)/shard_map/reduce_sum | solution.py:22
  207.1 0.0 copy-start.1
  207.1 1.3 copy-done.1
  208.4 0.0 copy-done.3
  208.4 0.8 convolution_bitcast_fusion
  209.2 0.0 copy-start.2
  209.2 1.3 copy-done.2
  210.5 0.9 slice.15
  211.4 2.0 copy.42
  213.4 1.5 collective-permute-start.2
  214.9 3.3 fusion.23
  218.2 1.6 copy.43
  219.8 17.9 %collective-permute-done.2 = bf16[256,1024]{1,0:T(8,128)(2,1)} collective-permute-done((bf16[256,1024]{1,0:T(8,128)(2,1)}, bf16[256,1024]{1,0:T(8,128)(2,1)}, u32[]{:S(2)}, u32[]{:S(2)}) %collective-permute-start.2) | collective-permute-done | bytes 524320 | tf_op jit(solution)/shard_map/ppermute | solution.py:15
  237.6 6.7 %convert_bitcast_fusion = bf16[4096,1024]{0,1:T(8,128)(2,1)} fusion(bf16[1,256,4096]{2,1,0:T(8,128)(2,1)S(1)} %copy-done, f32[256,1024]{1,0:T(8,128)S(1)} %copy.43, bf16[256,1024]{1,0:T(8,128)(2,1)} %collective-permute-done.2), kind=kOutput, calls=%fused_computation.4 | convolution fusion | flops 2152464384 | bytes 12058624 | tf_op jit(solution)/shard_map/tr,tc->rc/dot_general | solution.py:101
  244.3 0.0 reduce-scatter.5.cloned.1.call-update
  244.3 0.0 all-reduce.3.cloned.1.call-start
  244.4 156.7 %reduce-scatter.5.cloned.1.call-done = bf16[256,1024]{0,1:T(8,128)(2,1)} async-done(((bf16[4096,1024]{0,1:T(8,128)(2,1)}), bf16[256,1024]{0,1:T(8,128)(2,1)}) %reduce-scatter.5.cloned.1.call-update) | async-done | bytes 524304 | tf_op jit(solution)/shard_map/reduce_scatter | solution.py:100
  401.1 0.0 all-reduce.3.cloned.1.call-update
  401.1 0.6 multiply_reduce_fusion.1
  402.4 188.7 %psum.14 = f32[1]{0:T(128)} all-reduce(f32[1]{0:T(128)} %bitcast.9), channel_id=1, replica_groups=mesh['dp'=4,'ctx'=16,'tp'=4] {'ctx','tp'}, use_global_device_ids=true, to_apply=%region_7.8 | all-reduce | flops 1 | bytes 8 | tf_op jit(solution)/shard_map/psum | solution.py:109
  591.1 2.2 multiply_bitcast_fusion
  593.3 2.2 copy.44
  (5 shorter events, 0.0 us)
Async XLA Ops:
  7.2 165.3 %copy-start = (bf16[1,256,4096]{2,1,0:T(8,128)(2,1)S(1)}, bf16[1,256,4096]{2,1,0:T(8,128)(2,1)}, u32[]{:S(2)}) copy-start(bf16[1,256,4096]{2,1,0:T(8,128)(2,1)} %param.6) | copy-start | bytes 6291460
  12.7 159.8 %all-to-all-start = ((bf16[16,256,1024]{2,1,0:T(8,128)(2,1)}), bf16[16,256,1024]{2,1,0:T(8,128)(2,1)}, u32[]{:S(2)}, u32[]{:S(2)}) async-start(bf16[16,256,1024]{2,1,0:T(8,128)(2,1)} %stack.2), calls=%async_computation.1 | async-start | bytes 16777216 | tf_op jit(solution)/shard_map/all_to_all | solution.py:73
  19.6 56.5 %reduce-scatter.3.cloned.1.call-start = ((), (), s32[]{:S(2)}) async-start(), calls=%async_computation.3 | async-start | bytes 5242880 | tf_op jit(solution)/shard_map/reduce_scatter | solution.py:65
  26.1 54.1 %copy-start.4 = (s32[1,4096]{1,0:T(1,128)S(1)}, s32[1,4096]{1,0:T(1,128)}, u32[]{:S(2)}) copy-start(s32[1,4096]{1,0:T(1,128)} %param.8) | copy-start | bytes 49156
  26.1 375.0 %reduce-scatter.5.cloned.1.call-start = ((), (), s32[]{:S(2)}) async-start(), calls=%async_computation.4 | async-start | bytes 8912896 | tf_op jit(solution)/shard_map/reduce_scatter | solution.py:100
  76.1 57.2 %collective-permute-start = (bf16[256,2048]{0,1:T(8,128)(2,1)}, bf16[256,2048]{0,1:T(8,128)(2,1)S(1)}, u32[]{:S(2)}, u32[]{:S(2)}) collective-permute-start(bf16[256,2048]{0,1:T(8,128)(2,1)} %reduce-scatter.3.cloned.1.call-done), channel_id=1, source_target_pairs={{0,4},{4,8},{8,12},{12,16},{16,20},{20,24},{24,28},{28,32},{32,36}... | collective-permute-start | bytes 3145736 | tf_op jit(solution)/shard_map/ppermute | solution.py:15
  178.2 14.8 %collective-permute-start.1 = (bf16[256,1024]{1,0:T(8,128)(2,1)S(1)}, bf16[256,1024]{1,0:T(8,128)(2,1)S(1)}, u32[]{:S(2)}, u32[]{:S(2)}) collective-permute-start(bf16[256,1024]{1,0:T(8,128)(2,1)S(1)} %fusion.24), channel_id=1, source_target_pairs={{0,4},{4,8},{8,12},{12,16},{16,20},{20,24},{24,28},{28,32},{32,36}... | collective-permute-start | bytes 1572872 | tf_op jit(solution)/shard_map/ppermute | solution.py:15
  199.9 8.6 %copy-start.3 = (bf16[256,1024]{0,1:T(8,128)(2,1)S(1)}, bf16[256,1024]{0,1:T(8,128)(2,1)}, u32[]{:S(2)}) copy-start(bf16[256,1024]{0,1:T(8,128)(2,1)} %copy.50) | copy-start | bytes 1572868
  207.1 1.4 copy-start.1
  209.2 1.3 copy-start.2
  213.4 24.2 %collective-permute-start.2 = (bf16[256,1024]{1,0:T(8,128)(2,1)}, bf16[256,1024]{1,0:T(8,128)(2,1)}, u32[]{:S(2)}, u32[]{:S(2)}) collective-permute-start(bf16[256,1024]{1,0:T(8,128)(2,1)} %copy.42), channel_id=1, source_target_pairs={{4,0},{8,4},{12,8},{16,12},{20,16},{24,20},{28,24},{32,28},{36,32}... | collective-permute-start | bytes 1572872 | tf_op jit(solution)/shard_map/ppermute | solution.py:15
  244.3 349.0 %all-reduce.3.cloned.1.call-start = ((), (), s32[]{:S(2)}) async-start(), calls=%async_computation.5 | async-start | bytes 1048576 | tf_op jit(solution)/shard_map/psum | solution.py:108
Sparse Core Ops, SparseCore 0:
  26.2 49.8 reduce-scatter.2
  244.4 156.6 reduce-scatter.4
  403.8 54.1 all-reduce.2
